TPU v7x, 128 devices: a whole 4x4x4 slice. The times are simulated.
128 devices in a mesh: src: 4 (over y), row: 32 (over x, z, core).
Axes of the slice: x: 4, y: 4, z: 4, core: 2. Of those that a mesh axis runs over, the one named last changes fastest.
Arguments:
- load_root: bfloat16 [8192, 1536], P('row', 'src'), may hold values from -48 to 48
- load_branch: bfloat16 [2, 8192, 1536], P(None, 'row', 'src'), may hold values from -48 to 48
- load_leaf: bfloat16 [4, 4096, 1536], P(None, 'row', 'src'), may hold values from -48 to 48
- inverse_root: bfloat16 [8192, 8192], P('row'), may hold values from -1.5 to 1.5, as said below
- inverse_branch: bfloat16 [2, 8192, 8192], P(None, 'row'), may hold values from -1.5 to 1.5, as said below
- inverse_leaf: bfloat16 [4, 4096, 4096], P(None, 'row'), may hold values from -1.5 to 1.5, as said below
- coupling_branch: bfloat16 [2, 2048, 8192], P(None, None, 'row'), may hold values from -0.0625 to 0.0625
- coupling_leaf: bfloat16 [4, 2048, 4096], P(None, None, 'row'), may hold values from -0.09375 to 0.09375
- blocks_branch: int32 [2, 16], replicated, may hold values from 0 to 63, as said below
- blocks_leaf: int32 [4, 16], replicated, may hold values from 0 to 127, as said below
- parents: int32 [4], replicated, may hold values from 0 to 1, as said below
Outputs:
- field_root: float32 [8192, 1536], P('row', 'src')
- field_branch: float32 [2, 8192, 1536], P(None, 'row', 'src')
- field_leaf: float32 [4, 4096, 1536], P(None, 'row', 'src')
- coverage_root: float32 [8192], P('row')
- coverage_branch: float32 [2, 8192], P(None, 'row')
- coverage_leaf: float32 [4, 4096], P(None, 'row')
Inputs may be any that keep to these rules, and one draw needn't show every extreme that they name: `inverse_root`: lower triangular; diagonal entries between 0.5 and 1.5. `inverse_branch`: each block lower triangular; diagonal entries between 0.5 and 1.5. `inverse_leaf`: each block lower triangular; diagonal entries between 0.5 and 1.5. `blocks_branch`: each row holds distinct root block numbers. `blocks_leaf`: each row holds distinct numbers; its first 8 entries are below 8192/128 (parent blocks), the others are 64 or more (root blocks). `parents`: each of the two level-1 separators is the parent of exactly two level-2 separators.
All inputs are finite; a program needn't handle non-finite values.
Results may differ from a plain program's by a relative error of at most 0.0055.
Values may be sent and summed in bfloat16 or wider, within the bound.
A program may use at most 128 MiB of HBM per device.

v0:
```python
import jax
import jax.numpy as jnp
from jax import lax
from jax.sharding import PartitionSpec as P

ROOT_ROWS = 8192
BRANCH_ROWS = 8192
BLOCK_ROWS = 128
COUPLE_BLOCKS = 16


def place_blocks(values, node_ids, blocks, keep_count, first_block, node_total):
    relative = blocks - first_block
    inside = (relative >= 0) & (relative < keep_count)
    target = jnp.where(inside, node_ids * keep_count + relative, node_total * keep_count)
    buckets = jnp.zeros((node_total * keep_count,) + values.shape[1:], jnp.float32)
    buckets = buckets.at[target].add(values, mode="drop")
    return buckets.reshape(node_total, keep_count * values.shape[1], values.shape[2])


def solve_piece(inverse, part_rows):
    return jnp.einsum("nrw,nwc->nrc", inverse, part_rows, preferred_element_type=jnp.float32)


def local(
    load_root,
    load_branch,
    load_leaf,
    inverse_root,
    inverse_branch,
    inverse_leaf,
    coupling_branch,
    coupling_leaf,
    blocks_branch,
    blocks_leaf,
    parents,
):
    row_count = lax.axis_size("row")
    rank_index = lax.axis_index("row")
    source_count = load_leaf.shape[2]
    half_count = COUPLE_BLOCKS // 2
    half_rows = half_count * BLOCK_ROWS
    branch_blocks = BRANCH_ROWS // BLOCK_ROWS
    root_blocks = ROOT_ROWS // BLOCK_ROWS
    root_inverse = inverse_root[None]
    root_load = load_root[None]
    field_leaf = solve_piece(inverse_leaf, lax.all_gather(load_leaf, "row", axis=1, tiled=True))
    leaf_terms = jnp.einsum(
        "nrw,nwc->nrc",
        coupling_leaf,
        field_leaf.astype(jnp.bfloat16),
        preferred_element_type=jnp.float32,
    )
    parent_nodes = jnp.repeat(parents, half_count)
    parent_blocks = blocks_leaf[:, :half_count].reshape(-1)
    upper_blocks = (blocks_leaf[:, half_count:] - branch_blocks).reshape(-1)
    branch_targets = blocks_branch.reshape(-1)
    leaf_total = lax.psum(leaf_terms, "row")
    to_parent = leaf_total[:, :half_rows]
    to_root = leaf_total[:, half_rows:]
    parent_values = to_parent.reshape(-1, BLOCK_ROWS, source_count)
    own_blocks = branch_blocks // row_count
    branch_update = place_blocks(
        parent_values, parent_nodes, parent_blocks, own_blocks, rank_index * own_blocks, 2
    )
    branch_y = (load_branch.astype(jnp.float32) - branch_update).astype(jnp.bfloat16)
    field_branch = solve_piece(inverse_branch, lax.all_gather(branch_y, "row", axis=1, tiled=True))
    branch_terms = jnp.einsum(
        "nrw,nwc->nrc",
        coupling_branch,
        field_branch.astype(jnp.bfloat16),
        preferred_element_type=jnp.float32,
    )
    branch_total = lax.psum(branch_terms, "row")
    root_values = jnp.concatenate(
        [
            to_root.reshape(-1, BLOCK_ROWS, source_count),
            branch_total.reshape(-1, BLOCK_ROWS, source_count),
        ],
        axis=0,
    )
    root_targets = jnp.concatenate([upper_blocks, branch_targets], axis=0)
    root_nodes = jnp.zeros(root_targets.shape, jnp.int32)
    own_root = root_blocks // row_count
    root_update = place_blocks(
        root_values, root_nodes, root_targets, own_root, rank_index * own_root, 1
    )
    root_y = (root_load.astype(jnp.float32) - root_update).astype(jnp.bfloat16)
    field_root = solve_piece(root_inverse, lax.all_gather(root_y, "row", axis=1, tiled=True))
    field_root = field_root[0]
    coverage_root, coverage_branch, coverage_leaf = lax.psum(
        (
            jnp.sum(field_root * field_root, axis=-1),
            jnp.sum(field_branch * field_branch, axis=-1),
            jnp.sum(field_leaf * field_leaf, axis=-1),
        ),
        "src",
    )
    return (field_root, field_branch, field_leaf, coverage_root, coverage_branch, coverage_leaf)


def solution(mesh):
    return jax.shard_map(
        local,
        mesh=mesh,
        in_specs=(
            P("row", "src"),
            P(None, "row", "src"),
            P(None, "row", "src"),
            P("row", None),
            P(None, "row", None),
            P(None, "row", None),
            P(None, None, "row"),
            P(None, None, "row"),
            P(),
            P(),
            P(),
        ),
        out_specs=(
            P("row", "src"),
            P(None, "row", "src"),
            P(None, "row", "src"),
            P("row"),
            P(None, "row"),
            P(None, "row"),
        ),
        check_vma=False,
    )
```

profile of v0, /device:TPU:0, one launch (start us, length us, event | category | flops | bytes accessed | tf_op | source)
XLA Modules:
  0.0 562.4 jit_solution(9774117825941916616)
XLA Ops:
  7.2 0.0 copy-start
  7.2 0.0 all-gather.5.cloned.1.call-start
  7.2 0.7 all-gather.5.cloned.1.call-update
  7.9 0.0 all-reduce.4.cloned.1.call-start
  8.0 67.8 %all-gather.5.cloned.1.call-done = bf16[4,4096,384]{2,1,0:T(8,128)(2,1)} async-done(((bf16[4,128,384]{2,1,0:T(8,128)(2,1)}), bf16[4,4096,384]{2,1,0:T(8,128)(2,1)}) %all-gather.5.cloned.1.call-update) | async-done | bytes 12582928 | tf_op jit(solution)/shard_map/all_gather | solution.py:47
  75.8 8.3 %multiply_reduce_fusion = (f32[4,128]{1,0:T(4,128)S(1)}, f32[4,128,384]{2,1,0:T(8,128)S(1)}) fusion(bf16[4,128,4096]{2,1,0:T(8,128)(2,1)} %param.16, bf16[4,4096,384]{2,1,0:T(8,128)(2,1)} %all-gather.5.cloned.1.call-done), kind=kOutput, calls=%fused_computation.7 | convolution fusion | flops 1611005440 | bytes 17565696 | tf_op jit(solution)/shard_map/nrw,nwc->nrc/dot_general | solution.py:22
  84.1 6.3 %convolution_bitcast_fusion = f32[4,2048,384]{1,2,0:T(8,128)} fusion(bf16[4,2048,128]{2,1,0:T(8,128)(2,1)S(1)} %copy-done, f32[4,128,384]{2,1,0:T(8,128)S(1)} %get-tuple-element.30), kind=kOutput, calls=%fused_computation.3 | convolution fusion | flops 805502976 | bytes 15466496 | tf_op jit(solution)/shard_map/nrw,nwc->nrc/dot_general | solution.py:48
  90.4 0.0 all-reduce.4.cloned.1.call-update
  90.4 0.0 all-gather.7.cloned.1.call-start
  90.5 0.6 copy-done.8
  91.1 0.0 copy-done.6
  91.1 0.1 add_select_fusion
  91.2 0.1 select_n.48
  91.3 0.2 copy-done.4
  91.4 0.2 copy.23
  91.6 131.3 %all-reduce.4.cloned.1.call-done = f32[4,2048,384]{1,2,0:T(8,128)} async-done(((f32[4,2048,384]{1,2,0:T(8,128)}), f32[4,2048,384]{1,2,0:T(8,128)}) %all-reduce.4.cloned.1.call-update) | async-done | bytes 12582928 | tf_op jit(solution)/shard_map/psum | solution.py:58
  223.0 11.8 %fusion.5 = (f32[4,1024,384]{1,2,0:T(8,128)}, f32[4,1024,384]{1,2,0:T(8,128)}) fusion(f32[4,2048,384]{1,2,0:T(8,128)} %all-reduce.4.cloned.1.call-done), kind=kLoop, calls=%fused_computation.25 | loop fusion | bytes 25165824 | tf_op jit(solution)/shard_map/slice | solution.py:60
  234.8 6.6 %copy.24 = f32[4,1024,384]{2,1,0:T(8,128)} copy(f32[4,1024,384]{1,2,0:T(8,128)} %get-tuple-element.22) | data formatting | bytes 12582912 | tf_op jit(solution)/shard_map/slice | solution.py:59
  241.4 0.1 broadcast_in_dim.22
  241.4 9.8 %scatter_fusion = f32[4,128,384]{2,1,0:T(8,128)S(1)} fusion(f32[4,128,384]{2,1,0:T(8,128)S(1)} %broadcast_in_dim.22, s32[32]{0:T(128)S(1)} %fusion.4, f32[32,128,384]{2,1,0:T(8,128)} %bitcast.31), kind=kCustom, calls=%fused_computation | custom fusion | flops 1572864 | bytes 18874496 | tf_op jit(solution)/shard_map/scatter-add | solution.py:17
  251.3 0.3 copy.25
  251.5 0.8 subtract_convert_fusion
  252.4 0.0 all-gather.7.cloned.1.call-update
  252.4 0.0 copy-start.3
  252.4 0.0 all-reduce.6.cloned.1.call-start
  252.5 69.2 %all-gather.7.cloned.1.call-done = bf16[2,8192,384]{1,2,0:T(8,128)(2,1)} async-done(((bf16[2,256,384]{1,2,0:T(8,128)(2,1)}), bf16[2,8192,384]{1,2,0:T(8,128)(2,1)}) %all-gather.7.cloned.1.call-update) | async-done | bytes 12582928 | tf_op jit(solution)/shard_map/all_gather | solution.py:67
  321.6 11.1 %multiply_reduce_fusion.1 = (f32[2,256]{1,0:T(2,128)S(1)}, f32[2,256,384]{1,2,0:T(8,128)S(1)}) fusion(bf16[2,8192,384]{1,2,0:T(8,128)(2,1)} %all-gather.7.cloned.1.call-done, bf16[2,256,8192]{2,1,0:T(8,128)(2,1)} %param.15), kind=kOutput, calls=%fused_computation.8 | convolution fusion | flops 3221618176 | bytes 21760000 | tf_op jit(solution)/shard_map/nrw,nwc->nrc/dot_general | solution.py:22
  332.7 3.7 convolution_bitcast_fusion.1
  336.4 6.6 %copy.26 = f32[2,2048,384]{2,1,0:T(8,128)} copy(f32[2,2048,384]{1,2,0:T(8,128)} %convolution_bitcast_fusion.1) | data formatting | bytes 12582912 | tf_op jit(solution)/shard_map/nrw,nwc->nrc/dot_general | solution.py:68
  342.9 0.0 all-reduce.6.cloned.1.call-update
  343.0 0.2 all-gather.9.cloned.1.call-start
  343.2 0.1 concatenate.17
  343.3 0.3 copy-done.7
  343.6 0.1 concatenate.18
  343.7 0.1 fusion.3
  343.8 6.6 %copy.22 = f32[4,1024,384]{2,1,0:T(8,128)} copy(f32[4,1024,384]{1,2,0:T(8,128)} %get-tuple-element.21) | data formatting | bytes 12582912 | tf_op jit(solution)/shard_map/slice | solution.py:60
  350.4 108.2 %all-reduce.6.cloned.1.call-done = f32[32,128,384]{2,1,0:T(8,128)} async-done(((f32[32,128,384]{2,1,0:T(8,128)}), f32[32,128,384]{2,1,0:T(8,128)}) %all-reduce.6.cloned.1.call-update) | async-done | bytes 6291472 | tf_op jit(solution)/shard_map/psum | solution.py:74
  458.6 10.6 %pad_maximum_fusion = f32[64,128,384]{2,1,0:T(8,128)} fusion(f32[32,128,384]{2,1,0:T(8,128)} %all-reduce.6.cloned.1.call-done, f32[32,128,384]{2,1,0:T(8,128)} %bitcast.30), kind=kLoop, calls=%fused_computation.2 | loop fusion | flops 3145728 | bytes 25165824 | tf_op jit(solution)/shard_map/concatenate | solution.py:75
  469.3 0.0 copy-start.5
  469.3 19.1 %scatter_fusion.1 = f32[2,128,384]{2,1,0:T(8,128)S(1)} fusion(f32[2,128,384]{2,1,0:T(8,128)S(1)} %broadcast_in_dim.21, s32[64]{0:T(128)S(1)} %fusion.3, f32[64,128,384]{2,1,0:T(8,128)} %pad_maximum_fusion), kind=kCustom, calls=%fused_computation.1 | custom fusion | flops 3145728 | bytes 37748992 | tf_op jit(solution)/shard_map/scatter-add | solution.py:17
  488.4 0.7 fusion
  489.2 0.0 all-gather.9.cloned.1.call-update
  489.2 0.0 copy-start.1
  489.2 1.1 copy.28
  490.3 47.7 %all-gather.9.cloned.1.call-done = bf16[8192,384]{1,0:T(8,128)(2,1)} async-done(((bf16[256,384]{1,0:T(8,128)(2,1)}), bf16[8192,384]{1,0:T(8,128)(2,1)}) %all-gather.9.cloned.1.call-update) | async-done | bytes 6291472 | tf_op jit(solution)/shard_map/all_gather | solution.py:89
  538.0 5.8 %multiply_reduce_fusion.2 = (f32[256]{0:T(256)S(1)}, f32[256,384]{0,1:T(8,128)S(1)}) fusion(bf16[8192,384]{1,0:T(8,128)(2,1)} %all-gather.9.cloned.1.call-done, bf16[256,8192]{1,0:T(8,128)(2,1)} %param.14), kind=kOutput, calls=%fused_computation.12 | convolution fusion | flops 1610809088 | bytes 10880000 | tf_op jit(solution)/shard_map/nrw,nwc->nrc/dot_general | solution.py:22
  543.9 0.9 copy.27
  544.8 11.1 %all-reduce = (f32[256]{0:T(256)}, f32[2,256]{1,0:T(2,128)}, f32[4,128]{1,0:T(4,128)}) all-reduce(f32[256]{0:T(256)S(1)} %get-tuple-element.25, f32[2,256]{1,0:T(2,128)S(1)} %get-tuple-element.27, f32[4,128]{1,0:T(4,128)S(1)} %get-tuple-element.29), channel_id=1, replica_groups=mesh['src'=4,'row'=32] {'src'}, use_global_device_ids=true, to_apply=%region_5.6 | all-reduce | flops 1280 | bytes 10240 | tf_op jit(solution)/shard_map/psum | solution.py:91
  (13 shorter events, 0.1 us)
Async XLA Ops:
  7.2 76.9 %copy-start = (bf16[4,2048,128]{2,1,0:T(8,128)(2,1)S(1)}, bf16[4,2048,128]{2,1,0:T(8,128)(2,1)}, u32[]{:S(2)}) copy-start(bf16[4,2048,128]{2,1,0:T(8,128)(2,1)} %param.18) | copy-start | bytes 6291460
  7.2 68.6 %all-gather.5.cloned.1.call-start = ((), (), s32[]{:S(2)}) async-start(), calls=%async_computation | async-start | bytes 12976128 | tf_op jit(solution)/shard_map/all_gather | solution.py:47
  7.9 215.0 %all-reduce.4.cloned.1.call-start = ((), (), s32[]{:S(2)}) async-start(), calls=%async_computation.1 | async-start | bytes 25165824 | tf_op jit(solution)/shard_map/psum | solution.py:58
  84.1 6.3 %copy-start.2 = (f32[4,128,384]{2,1,0:T(8,128)}, f32[4,128,384]{2,1,0:T(8,128)S(1)}, u32[]{:S(2)}) copy-start(f32[4,128,384]{2,1,0:T(8,128)S(1)} %get-tuple-element.30) | copy-start | bytes 2359300
  90.4 0.7 copy-start.8
  90.4 0.7 copy-start.6
  90.4 1.0 copy-start.4
  90.4 231.2 %all-gather.7.cloned.1.call-start = ((), (), s32[]{:S(2)}) async-start(), calls=%async_computation.2 | async-start | bytes 12976128 | tf_op jit(solution)/shard_map/all_gather | solution.py:67
  252.4 80.3 %copy-start.3 = (bf16[2,2048,256]{2,1,0:T(8,128)(2,1)S(1)}, bf16[2,2048,256]{2,1,0:T(8,128)(2,1)}, u32[]{:S(2)}) copy-start(bf16[2,2048,256]{2,1,0:T(8,128)(2,1)} %param.17) | copy-start | bytes 6291460
  252.4 206.2 %all-reduce.6.cloned.1.call-start = ((), (), s32[]{:S(2)}) async-start(), calls=%async_computation.3 | async-start | bytes 12582912 | tf_op jit(solution)/shard_map/psum | solution.py:74
  342.9 0.7 copy-start.7
  343.0 195.0 %all-gather.9.cloned.1.call-start = ((), (), s32[]{:S(2)}) async-start(), calls=%async_computation.4 | async-start | bytes 6488064 | tf_op jit(solution)/shard_map/all_gather | solution.py:89
  469.3 19.1 %copy-start.5 = (bf16[256,384]{1,0:T(8,128)(2,1)S(1)}, bf16[256,384]{1,0:T(8,128)(2,1)}, u32[]{:S(2)}) copy-start(bf16[256,384]{1,0:T(8,128)(2,1)} %param.11) | copy-start | bytes 589828
  489.2 66.7 %copy-start.1 = (bf16[4,2048,128]{2,1,0:T(8,128)(2,1)S(1)}, bf16[4,2048,128]{2,1,0:T(8,128)(2,1)}, u32[]{:S(2)}) copy-start(bf16[4,2048,128]{2,1,0:T(8,128)(2,1)} %param.18) | copy-start | bytes 6291460
Sparse Core Ops, SparseCore 0:
  10.3 65.4 all-gather.4
  90.6 132.3 all-reduce.3
  252.5 69.0 all-gather.6
  343.1 115.5 all-reduce.5
  489.3 48.6 all-gather.8
where the time goes:
time: 563 us; the launch traced here: 562 us
  waiting for transfers between devices  425 us (75%)
  other arithmetic  41.3 us (7%)
  local copies, waits for them, and re-layouts  35.6 us (6%)
  matrix products  35.2 us (6%)
  between operations  13.9 us (2%)
  blocking collectives  11.1 us (2%)
    psum x1, waiting for transfers between devices, local(): leaf_total = lax.psum(leaf_terms, 'row')  131 us
    psum x1, waiting for transfers between devices, local(): branch_total = lax.psum(branch_terms, 'row')  108 us
    all_gather x1, waiting for transfers between devices, local(): lax.all_gather(branch_y, 'row', axis=1, tiled=True)  69.2 us
    all_gather x1, waiting for transfers between devices, local(): lax.all_gather(load_leaf, 'row', axis=1, tiled=True)  67.8 us
    all_gather x1, waiting for transfers between devices, local(): lax.all_gather(root_y, 'row', axis=1, tiled=True)  47.7 us
    scatter-add x2, other arithmetic, place_blocks(): buckets = buckets.at[target].add(values, mode='drop')  28.9 us
    dot_general x3, matrix products, solve_piece(): jnp.einsum('nrw,nwc->nrc', inverse, part_rows, preferred_element_type=jnp...  25.2 us
    slice x2, local copies, waits for them, and re-layouts, local(): to_root = leaf_total[:, half_rows:]  18.5 us
  transfers between devices with their start and end apart: 5, of which 5 were waited for; matrix products, arithmetic and copies ran while one was open for 1% of the time, Pallas kernels for 0%

commit v1 on v0

--- a/solution.py
+++ b/solution.py
@@ -1,3 +1,4 @@
+import functools
 import jax
 import jax.numpy as jnp
 from jax import lax
@@ -7,6 +8,18 @@
 BRANCH_ROWS = 8192
 BLOCK_ROWS = 128
 COUPLE_BLOCKS = 16
+
+
+def take_the_area(arr_in, group_axis):
+    fan = lax.axis_size(group_axis)
+    ready = arr_in
+    raw_out = lambda lower: [(nth, nth ^ lower) for nth in range(fan)]
+    for q in range(fan.bit_length() - 1):
+        ready = ready + lax.ppermute(ready, axis_name=group_axis, perm=raw_out(1 << q))
+    return ready
+
+
+detail_strips_all_by_axis = functools.partial(take_the_area, group_axis="row")
 
 
 def place_blocks(values, node_ids, blocks, keep_count, first_block, node_total):
@@ -71,7 +84,7 @@
         field_branch.astype(jnp.bfloat16),
         preferred_element_type=jnp.float32,
     )
-    branch_total = lax.psum(branch_terms, "row")
+    branch_total = detail_strips_all_by_axis(branch_terms)
     root_values = jnp.concatenate(
         [
             to_root.reshape(-1, BLOCK_ROWS, source_count),

time: 563 us -> 1030 us (1.83)
  waiting for transfers between devices: 425 us -> 863 us
  other arithmetic: 41.3 us -> 66.6 us
    ppermute x0 -> x5, waiting for transfers between devices: none -> 546 us  [take_the_area(): lax.ppermute(ready, axis_name=group_axis, perm=raw_out(1 << q))]
    psum x1 -> x0, waiting for transfers between devices: 108 us -> none  [local(): branch_total = lax.psum(branch_terms, 'row')]
    add x0 -> x5, other arithmetic: none -> 25.4 us  [take_the_area(): ready + lax.ppermute(ready, axis_name=group_axis, perm=raw_out(1 << q))]
  transfers between devices with their start and end apart: 5 -> 9, of which waited for: 5 -> 9; matrix products, arithmetic and copies ran while one was open for 1% -> 1% of each run, Pallas kernels for 0% -> 0%
where the time goes in v1:
time: 1030 us
  waiting for transfers between devices  863 us (84%)
  other arithmetic  66.6 us (6%)
  local copies, waits for them, and re-layouts  35.2 us (3%)
  matrix products  32.6 us (3%)
  between operations  13.9 us (1%)
  blocking collectives  11.1 us (1%)
    ppermute x5, waiting for transfers between devices, take_the_area(): lax.ppermute(ready, axis_name=group_axis, perm=raw_out(1 << q))  546 us
    psum x1, waiting for transfers between devices, local(): leaf_total = lax.psum(leaf_terms, 'row')  131 us
    all_gather x1, waiting for transfers between devices, local(): lax.all_gather(branch_y, 'row', axis=1, tiled=True)  69.2 us
    all_gather x1, waiting for transfers between devices, local(): lax.all_gather(load_leaf, 'row', axis=1, tiled=True)  67.8 us
    all_gather x1, waiting for transfers between devices, local(): lax.all_gather(root_y, 'row', axis=1, tiled=True)  47.9 us
    scatter-add x2, other arithmetic, place_blocks(): buckets = buckets.at[target].add(values, mode='drop')  28.9 us
    add x5, other arithmetic, take_the_area(): ready + lax.ppermute(ready, axis_name=group_axis, perm=raw_out(1 << q))  25.4 us
    dot_general x3, matrix products, solve_piece(): jnp.einsum('nrw,nwc->nrc', inverse, part_rows, preferred_element_type=jnp...  25.2 us
  transfers between devices with their start and end apart: 9, of which 9 were waited for; matrix products, arithmetic and copies ran while one was open for 1% of the time, Pallas kernels for 0%

profile of v1, /device:TPU:0, one launch (start us, length us, event | category | flops | bytes accessed | tf_op | source)
XLA Modules:
  0.0 1029.5 jit_solution(11038600576329997613)
XLA Ops:
  7.2 0.7 all-gather.5.cloned.1.call-update
  8.0 67.8 %all-gather.5.cloned.1.call-done = bf16[4,4096,384]{2,1,0:T(8,128)(2,1)} async-done(((bf16[4,128,384]{2,1,0:T(8,128)(2,1)}), bf16[4,4096,384]{2,1,0:T(8,128)(2,1)}) %all-gather.5.cloned.1.call-update) | async-done | bytes 12582928 | tf_op jit(solution)/shard_map/all_gather | solution.py:60
  75.8 8.3 multiply_reduce_fusion
  84.1 6.3 convolution_bitcast_fusion
  90.4 0.0 all-gather.7.cloned.1.call-start
  90.5 0.6 copy-done.8
  91.1 0.1 add_select_fusion
  91.2 0.1 select_n.48
  91.3 0.2 copy-done.4
  91.4 0.2 copy.23
  91.6 131.3 %all-reduce.3.cloned.1.call-done = f32[4,2048,384]{1,2,0:T(8,128)} async-done(((f32[4,2048,384]{1,2,0:T(8,128)}), f32[4,2048,384]{1,2,0:T(8,128)}) %all-reduce.3.cloned.1.call-update) | async-done | bytes 12582928 | tf_op jit(solution)/shard_map/psum | solution.py:71
  223.0 11.8 %fusion.5 = (f32[4,1024,384]{1,2,0:T(8,128)}, f32[4,1024,384]{1,2,0:T(8,128)}) fusion(f32[4,2048,384]{1,2,0:T(8,128)} %all-reduce.3.cloned.1.call-done), kind=kLoop, calls=%fused_computation.25 | loop fusion | bytes 25165824 | tf_op jit(solution)/shard_map/slice | solution.py:73
  234.8 6.6 copy.24
  241.4 0.1 broadcast_in_dim.22
  241.4 9.8 scatter_fusion
  251.2 0.3 copy.25
  251.5 0.8 subtract_convert_fusion
  252.4 69.2 %all-gather.7.cloned.1.call-done = bf16[2,8192,384]{1,2,0:T(8,128)(2,1)} async-done(((bf16[2,256,384]{1,2,0:T(8,128)(2,1)}), bf16[2,8192,384]{1,2,0:T(8,128)(2,1)}) %all-gather.7.cloned.1.call-update) | async-done | bytes 12582928 | tf_op jit(solution)/shard_map/all_gather | solution.py:80
  321.6 11.1 %multiply_reduce_fusion.1 = (f32[2,256]{1,0:T(2,128)S(1)}, f32[2,256,384]{1,2,0:T(8,128)S(1)}) fusion(bf16[2,8192,384]{1,2,0:T(8,128)(2,1)} %all-gather.7.cloned.1.call-done, bf16[2,256,8192]{2,1,0:T(8,128)(2,1)} %param.15), kind=kOutput, calls=%fused_computation.8 | convolution fusion | flops 3221618176 | bytes 21760000 | tf_op jit(solution)/shard_map/nrw,nwc->nrc/dot_general | solution.py:35
  332.7 1.0 convolution_bitcast_fusion.1
  333.7 0.5 collective-permute-start
  334.2 10.0 collective-permute-done
  344.3 4.1 add.63
  348.3 1.3 collective-permute-start.1
  349.6 136.6 %collective-permute-done.1 = f32[2,2048,384]{1,2,0:T(8,128)} collective-permute-done((f32[2,2048,384]{1,2,0:T(8,128)S(1)}, f32[2,2048,384]{1,2,0:T(8,128)}, u32[]{:S(2)}, u32[]{:S(2)}) %collective-permute-start.1) | collective-permute-done | bytes 6291488 | tf_op jit(solution)/shard_map/ppermute | solution.py:18
  486.2 4.1 add.64
  490.3 2.2 collective-permute-start.2
  492.5 136.3 %collective-permute-done.2 = f32[2,2048,384]{1,2,0:T(8,128)} collective-permute-done((f32[2,2048,384]{1,2,0:T(8,128)S(1)}, f32[2,2048,384]{1,2,0:T(8,128)}, u32[]{:S(2)}, u32[]{:S(2)}) %collective-permute-start.2) | collective-permute-done | bytes 6291488 | tf_op jit(solution)/shard_map/ppermute | solution.py:18
  628.8 4.1 add.65
  632.9 1.3 collective-permute-start.3
  634.1 134.8 %collective-permute-done.3 = f32[2,2048,384]{1,2,0:T(8,128)S(1)} collective-permute-done((f32[2,2048,384]{1,2,0:T(8,128)S(1)}, f32[2,2048,384]{1,2,0:T(8,128)S(1)}, u32[]{:S(2)}, u32[]{:S(2)}) %collective-permute-start.3) | collective-permute-done | bytes 6291488 | tf_op jit(solution)/shard_map/ppermute | solution.py:18
  768.9 3.9 add.66
  772.9 2.0 collective-permute-start.4
  774.9 0.1 concatenate.17
  775.0 0.1 concatenate.18
  775.0 0.1 fusion.3
  775.1 6.6 copy.22
  781.7 128.1 %collective-permute-done.4 = f32[2,2048,384]{1,2,0:T(8,128)} collective-permute-done((f32[2,2048,384]{1,2,0:T(8,128)}, f32[2,2048,384]{1,2,0:T(8,128)}, u32[]{:S(2)}, u32[]{:S(2)}) %collective-permute-start.4) | collective-permute-done | bytes 6291488 | tf_op jit(solution)/shard_map/ppermute | solution.py:18
  909.8 9.2 add.67
  919.0 6.6 copy.26
  925.5 10.6 %pad_maximum_fusion = f32[64,128,384]{2,1,0:T(8,128)} fusion(f32[32,128,384]{2,1,0:T(8,128)} %bitcast.31, f32[32,128,384]{2,1,0:T(8,128)} %bitcast.29), kind=kLoop, calls=%fused_computation.2 | loop fusion | flops 3145728 | bytes 25165824 | tf_op jit(solution)/shard_map/concatenate | solution.py:88
  936.2 19.1 %scatter_fusion.1 = f32[2,128,384]{2,1,0:T(8,128)S(1)} fusion(f32[2,128,384]{2,1,0:T(8,128)S(1)} %broadcast_in_dim.21, s32[64]{0:T(128)S(1)} %fusion.3, f32[64,128,384]{2,1,0:T(8,128)} %pad_maximum_fusion), kind=kCustom, calls=%fused_computation.1 | custom fusion | flops 3145728 | bytes 37748992 | tf_op jit(solution)/shard_map/scatter-add | solution.py:30
  955.3 0.7 fusion
  956.1 1.1 copy.28
  957.2 47.9 %all-gather.9.cloned.1.call-done = bf16[8192,384]{1,0:T(8,128)(2,1)} async-done(((bf16[256,384]{1,0:T(8,128)(2,1)}), bf16[8192,384]{1,0:T(8,128)(2,1)}) %all-gather.9.cloned.1.call-update) | async-done | bytes 6291472 | tf_op jit(solution)/shard_map/all_gather | solution.py:102
  1005.1 5.8 multiply_reduce_fusion.2
  1011.0 0.9 copy.27
  1011.9 11.1 %all-reduce = (f32[256]{0:T(256)}, f32[2,256]{1,0:T(2,128)}, f32[4,128]{1,0:T(4,128)}) all-reduce(f32[256]{0:T(256)S(1)} %get-tuple-element.25, f32[2,256]{1,0:T(2,128)S(1)} %get-tuple-element.27, f32[4,128]{1,0:T(4,128)S(1)} %get-tuple-element.29), channel_id=1, replica_groups=mesh['src'=4,'row'=32] {'src'}, use_global_device_ids=true, to_apply=%region_4.5 | all-reduce | flops 1280 | bytes 10240 | tf_op jit(solution)/shard_map/psum | solution.py:104
  (25 shorter events, 0.3 us)
Async XLA Ops:
  7.2 76.9 %copy-start = (bf16[4,2048,128]{2,1,0:T(8,128)(2,1)S(1)}, bf16[4,2048,128]{2,1,0:T(8,128)(2,1)}, u32[]{:S(2)}) copy-start(bf16[4,2048,128]{2,1,0:T(8,128)(2,1)} %param.18) | copy-start | bytes 6291460
  7.2 68.6 %all-gather.5.cloned.1.call-start = ((), (), s32[]{:S(2)}) async-start(), calls=%async_computation | async-start | bytes 12976128 | tf_op jit(solution)/shard_map/all_gather | solution.py:60
  7.9 215.0 %all-reduce.3.cloned.1.call-start = ((), (), s32[]{:S(2)}) async-start(), calls=%async_computation.1 | async-start | bytes 25165824 | tf_op jit(solution)/shard_map/psum | solution.py:71
  84.1 6.3 copy-start.2
  90.4 0.7 copy-start.8
  90.4 0.7 copy-start.6
  90.4 1.0 copy-start.4
  90.4 231.1 %all-gather.7.cloned.1.call-start = ((), (), s32[]{:S(2)}) async-start(), calls=%async_computation.2 | async-start | bytes 12976128 | tf_op jit(solution)/shard_map/all_gather | solution.py:80
  252.4 80.3 %copy-start.3 = (bf16[2,2048,256]{2,1,0:T(8,128)(2,1)S(1)}, bf16[2,2048,256]{2,1,0:T(8,128)(2,1)}, u32[]{:S(2)}) copy-start(bf16[2,2048,256]{2,1,0:T(8,128)(2,1)} %param.17) | copy-start | bytes 6291460
  252.4 752.7 %all-gather.9.cloned.1.call-start = ((), (), s32[]{:S(2)}) async-start(), calls=%async_computation.3 | async-start | bytes 6488064 | tf_op jit(solution)/shard_map/all_gather | solution.py:102
  333.7 10.6 %collective-permute-start = (f32[2,2048,384]{1,2,0:T(8,128)S(1)}, f32[2,2048,384]{1,2,0:T(8,128)}, u32[]{:S(2)}, u32[]{:S(2)}) collective-permute-start(f32[2,2048,384]{1,2,0:T(8,128)S(1)} %convolution_bitcast_fusion.1), channel_id=1, source_target_pairs={{0,1},{1,0},{2,3},{3,2},{4,5},{5,4},{6,7},{7,6},{8,9},{9,8},{10,11... | collective-permute-start | bytes 18874376 | tf_op jit(solution)/shard_map/ppermute | solution.py:18
  348.3 137.9 %collective-permute-start.1 = (f32[2,2048,384]{1,2,0:T(8,128)S(1)}, f32[2,2048,384]{1,2,0:T(8,128)}, u32[]{:S(2)}, u32[]{:S(2)}) collective-permute-start(f32[2,2048,384]{1,2,0:T(8,128)S(1)} %add.63), channel_id=1, source_target_pairs={{0,2},{1,3},{2,0},{3,1},{4,6},{5,7},{6,4},{7,5},{8,10},{9,11},{10,... | collective-permute-start | bytes 18874376 | tf_op jit(solution)/shard_map/ppermute | solution.py:18
  490.3 138.5 %collective-permute-start.2 = (f32[2,2048,384]{1,2,0:T(8,128)S(1)}, f32[2,2048,384]{1,2,0:T(8,128)}, u32[]{:S(2)}, u32[]{:S(2)}) collective-permute-start(f32[2,2048,384]{1,2,0:T(8,128)S(1)} %add.64), channel_id=1, source_target_pairs={{0,4},{1,5},{2,6},{3,7},{4,0},{5,1},{6,2},{7,3},{8,12},{9,13},{10,... | collective-permute-start | bytes 18874376 | tf_op jit(solution)/shard_map/ppermute | solution.py:18
  632.9 142.1 %copy-start.7 = (s32[2,16]{1,0:T(2,128)S(1)}, s32[2,16]{1,0:T(2,128)}, u32[]{:S(2)}) copy-start(s32[2,16]{1,0:T(2,128)} %param.19) | copy-start | bytes 388
  632.9 136.0 %collective-permute-start.3 = (f32[2,2048,384]{1,2,0:T(8,128)S(1)}, f32[2,2048,384]{1,2,0:T(8,128)S(1)}, u32[]{:S(2)}, u32[]{:S(2)}) collective-permute-start(f32[2,2048,384]{1,2,0:T(8,128)S(1)} %add.65), channel_id=1, source_target_pairs={{0,8},{1,9},{2,10},{3,11},{4,12},{5,13},{6,14},{7,15},{8,0},{9,1},... | collective-permute-start | bytes 18874376 | tf_op jit(solution)/shard_map/ppermute | solution.py:18
  772.9 136.9 %collective-permute-start.4 = (f32[2,2048,384]{1,2,0:T(8,128)}, f32[2,2048,384]{1,2,0:T(8,128)}, u32[]{:S(2)}, u32[]{:S(2)}) collective-permute-start(f32[2,2048,384]{1,2,0:T(8,128)} %add.66), channel_id=1, source_target_pairs={{0,16},{1,17},{2,18},{3,19},{4,20},{5,21},{6,22},{7,23},{8,24},{9,... | collective-permute-start | bytes 18874376 | tf_op jit(solution)/shard_map/ppermute | solution.py:18
  936.2 19.1 %copy-start.5 = (bf16[256,384]{1,0:T(8,128)(2,1)S(1)}, bf16[256,384]{1,0:T(8,128)(2,1)}, u32[]{:S(2)}) copy-start(bf16[256,384]{1,0:T(8,128)(2,1)} %param.11) | copy-start | bytes 589828
  956.0 67.0 %copy-start.1 = (bf16[4,2048,128]{2,1,0:T(8,128)(2,1)S(1)}, bf16[4,2048,128]{2,1,0:T(8,128)(2,1)}, u32[]{:S(2)}) copy-start(bf16[4,2048,128]{2,1,0:T(8,128)(2,1)} %param.18) | copy-start | bytes 6291460
Sparse Core Ops, SparseCore 0:
  10.3 65.4 all-gather.4
  90.6 132.3 all-reduce.2
  252.5 69.0 all-gather.6
  956.2 48.9 all-gather.8
